TPU v7x, 32 devices: a whole 2x2x4 slice. The times are simulated.
32 devices in a mesh: ctx: 16 (over z, x, core), head: 2 (over y).
Axes of the slice: x: 2, y: 2, z: 4, core: 2. Of those that a mesh axis runs over, the one named last changes fastest.
Arguments:
- q_absorbed: bfloat16 [2048, 64, 576], P('ctx', 'head'), may hold values from -6 to 6
- grad_out: bfloat16 [2048, 64, 512], P('ctx', 'head'), may hold values from -6 to 6
- log_norm: float32 [2048, 64], P('ctx', 'head'), may hold values from 5 to 7
- out_dot: float32 [2048, 64], P('ctx', 'head'), may hold values from -6 to 6
- kv_cache: bfloat16 [2048, 576], P(('ctx', 'head')), may hold values from -6 to 6
- block_links: int32 [16, 4], P('ctx'), may hold values 0 or 1
Outputs:
- d_query: bfloat16 [2048, 64, 576], P('ctx', 'head')
- d_kv: bfloat16 [2048, 576], P(('ctx', 'head'))
All inputs are finite; a program needn't handle non-finite values. No bound on the sum of `block_links` on one device may be relied on, other than what follows from the above.
Results may differ from a plain program's by a relative error of at most 0.0061.
Values may be sent and summed in bfloat16 or wider, within the bound.
A program may use at most 128 MiB of HBM per device.

v0:
```python
import functools
import math

import jax
import jax.numpy as jnp
from jax import lax
from jax.experimental import pallas as pl
from jax.experimental.pallas import tpu as pltpu
from jax.sharding import PartitionSpec as P

offset_list = (0, 1, 2, 8)
F32 = jnp.float32
BF16 = jnp.bfloat16


def dot(a, b, ca, cb):
    return lax.dot_general(a, b, (((ca,), (cb,)), ((), ())), preferred_element_type=F32)


MESH = pl.DeviceIdType.MESH
FIRST, LAST = (0, 2), (2, 4)


def fused_kernel(
    n_ctx, n_head, links, kv_ref, q_hbm, g_hbm, ln_ref, od_ref,
    dq_hbm, dkv_ref,
    qv, graw, gwide, gv, dsv, pbv, dqv, acc, kvbuf, away, yrecv, fwd, crecv,
    q_sem, g_sem, dq_sem, gs_s, gs_r, fw_s, fw_r, ry_s, ry_r, rc_s, rc_r,
):
    me = lax.axis_index("ctx")
    head = lax.axis_index("head")
    steps, group, feat, toks = qv.shape
    chunks, width, heads, lat = graw.shape
    cols = group * toks
    n_off, _, part, _ = kvbuf.shape
    blk = n_head * part
    scale = feat ** (-0.5)
    log2e = math.log2(math.e)

    def load_g(i):
        return pltpu.make_async_copy(g_hbm.at[pl.ds(i * width, width)], graw.at[i], g_sem.at[i])

    def load_q(i):
        return pltpu.make_async_copy(q_hbm.at[pl.ds(i * group, group)], qv.at[i], q_sem.at[i])

    def store_dq(i):
        return pltpu.make_async_copy(dqv.at[i], dq_hbm.at[pl.ds(i * group, group)], dq_sem.at[i])

    def loop(count, body):
        def run(i, carry):
            body(i)
            return carry

        lax.fori_loop(0, count, run, 0)

    def at_ctx(by):
        return (lax.rem(me + by + n_ctx, n_ctx), head)

    def at_head(by):
        return (me, lax.rem(head + by + n_head, n_head))

    def send(src, dst, s_sem, r_sem, where):
        return pltpu.make_async_remote_copy(
            src_ref=src, dst_ref=dst, send_sem=s_sem, recv_sem=r_sem, device_id=where, device_id_type=MESH
        )

    loop(chunks, lambda i: load_g(i).start())

    away_by = sorted({by % n_ctx for o in offset_list[1:] for by in (o, -o)})
    barrier = pltpu.get_barrier_semaphore()
    for by in away_by:
        pl.semaphore_signal(barrier, inc=1, device_id=at_ctx(by), device_id_type=MESH)
    for j in range(1, n_head):
        pl.semaphore_signal(barrier, inc=1, device_id=at_head(j), device_id_type=MESH)
    pl.semaphore_wait(barrier, len(away_by) + n_head - 1)

    gather = [
        send(kv_ref, kvbuf.at[pos, 0], gs_s.at[pos - 1], gs_r.at[pos - 1], at_ctx(offset_list[pos]))
        for pos in range(1, n_off)
    ]
    spread = [
        [
            send(kv_ref if pos == 0 else kvbuf.at[pos, 0], kvbuf.at[pos, j],
                 fw_s.at[pos, j - 1], fw_r.at[pos, j - 1], at_head(-j))
            for j in range(1, n_head)
        ]
        for pos in range(n_off)
    ]
    for copy in gather:
        copy.start()
    for copy in spread[0]:
        copy.start()
    loop(steps, lambda i: load_q(i).start())
    kvbuf[0, 0] = kv_ref[...]

    def relayout(i):
        load_g(i).wait()
        wide = graw[i].reshape(width * heads, lat).astype(F32)
        lanes = gwide.shape[2]
        for c in range(gwide.shape[0]):
            gwide[c] = wide[:, c * lanes : (c + 1) * lanes]
        for h in range(heads):
            for c in range(gwide.shape[0]):
                gv[h // group, h % group, pl.ds(i * width, width), c * lanes : (c + 1) * lanes] = gwide[
                    c, pl.ds(h, width, stride=heads), :
                ].astype(BF16)

    loop(chunks, relayout)

    def scores(i, low, high):
        keys = kvbuf[low:high].reshape((high - low) * blk, feat)
        q = jnp.concatenate([qv[i, k] for k in range(group)], 1)
        g = gv[i].reshape(cols, lat)
        ln = jnp.concatenate([ln_ref[i, k : k + 1, :] for k in range(group)], 1) * log2e
        od = jnp.concatenate([od_ref[i, k : k + 1, :] for k in range(group)], 1)
        s = dot(keys, q, 1, 0)
        dp = dot(keys[:, :lat], g, 1, 1)
        ps, dss = [], []
        for pos in range(low, high):
            sl = slice((pos - low) * blk, (pos - low + 1) * blk)
            bias = jnp.where(links[0, pos] > 0, ln, 1e30)
            p = jnp.exp2(s[sl] * (scale * log2e) - bias)
            if offset_list[pos] == 0:
                key = lax.broadcasted_iota(jnp.int32, p.shape, 0) + head * part
                key = jnp.where(key >= blk, key - blk, key)
                tok = lax.rem(lax.broadcasted_iota(jnp.int32, p.shape, 1), toks)
                p = jnp.where(tok >= key, p, 0.0)
            ps.append(p.astype(BF16))
            dss.append((p * (dp[sl] - od) * scale).astype(BF16))
        return jnp.concatenate(ps, 0), jnp.concatenate(dss, 0), q, g

    def key_terms(pb, ds, q, g, low, high):
        rows = slice(low * blk, high * blk)
        dk = dot(ds, q, 1, 1)
        dv = dot(pb, g, 1, 0)
        acc[rows, :lat] += dk[:, :lat] + dv
        acc[rows, lat:] += dk[:, lat:]

    def across(low, high, slot):
        return [
            send(away.at[j - 1, low:high], yrecv.at[j - 1, low:high], ry_s.at[slot, j - 1],
                 ry_r.at[slot, j - 1], at_head(j))
            for j in range(1, n_head)
        ]

    def pack(low, high):
        for pos in range(low, high):
            for j in range(1, n_head):
                start = pos * blk + j * part
                away[j - 1, pos] = acc[start : start + part, :].astype(BF16)

    def folded(pos):
        total = acc[pos * blk : pos * blk + part, :]
        for j in range(1, n_head):
            total = total + yrecv[j - 1, pos].astype(F32)
        return total

    back = [
        send(fwd.at[pos - 1], crecv.at[pos - 1], rc_s.at[pos - 1], rc_r.at[pos - 1], at_ctx(-offset_list[pos]))
        for pos in range(1, n_off)
    ]

    acc[...] = jnp.zeros_like(acc)
    for pos in range(1, n_off):
        if pos == FIRST[1]:
            arrive(spread, FIRST)
            first_scores(loop, steps, load_q, scores, dsv, pbv, blk)
        gather[pos - 1].wait_recv()
        for copy in spread[pos]:
            copy.start()
    arrive(spread, LAST)

    def second(i):
        pb, ds, q, g = scores(i, *LAST)
        dsv[i, LAST[0] * blk : LAST[1] * blk, :] = ds
        key_terms(pb, ds, q, g, *LAST)

    loop(steps, second)
    pack(*LAST)

    def third(i):
        q = jnp.concatenate([qv[i, k] for k in range(group)], 1)
        key_terms(pbv[i], dsv[i, : FIRST[1] * blk, :], q, gv[i].reshape(cols, lat), *FIRST)

    def fourth(i):
        keys = kvbuf[...].reshape(n_off * blk, feat)
        dq = dot(keys, dsv[i], 0, 0).astype(BF16)
        for k in range(group):
            dqv[i, k] = dq[:, k * toks : (k + 1) * toks]
        store_dq(i).start()

    far, near = across(*LAST, 1), across(*FIRST, 0)
    for copy in far:
        copy.start()
    loop(steps, third)
    for copy in far:
        copy.wait_recv()
    for pos in range(*LAST):
        fwd[pos - 1] = folded(pos).astype(BF16)
    pack(*FIRST)
    for pos in range(*LAST):
        back[pos - 1].start()
    for copy in near:
        copy.start()
    loop(steps, fourth)
    for copy in near:
        copy.wait_recv()
    for pos in range(1, FIRST[1]):
        fwd[pos - 1] = folded(pos).astype(BF16)
    total = folded(0)
    for pos in range(1, FIRST[1]):
        back[pos - 1].start()
    loop(steps, lambda i: store_dq(i).wait())
    for copy in gather + sum(spread, []) + far + near:
        copy.wait_send()
    for copy in back[::-1]:
        copy.wait()
    for pos in range(1, n_off):
        total = total + crecv[pos - 1].astype(F32)
    dkv_ref[...] = total.astype(BF16)


def arrive(spread, span):
    for pos in range(*span):
        for copy in spread[pos]:
            copy.wait_recv()


def first_scores(loop, steps, load_q, scores, dsv, pbv, blk):
    def first(i):
        load_q(i).wait()
        pb, ds, _, _ = scores(i, *FIRST)
        dsv[i, : FIRST[1] * blk, :] = ds
        pbv[i] = pb

    loop(steps, first)


def fused(n_ctx, n_head, q, g, ln, od, kv, links, group=4, width=32):
    heads, feat, toks = q.shape
    lat = g.shape[2]
    part = kv.shape[0]
    n_off = len(offset_list)
    group = math.gcd(group, heads)
    width = math.gcd(width, toks)
    steps, chunks = heads // group, toks // width
    cols, keys = group * toks, n_off * n_head * part
    near = FIRST[1] * n_head * part
    dma = pltpu.SemaphoreType.DMA
    hbm = pl.BlockSpec(memory_space=pl.ANY)
    vmem = pl.BlockSpec(memory_space=pltpu.VMEM)
    return pl.pallas_call(
        functools.partial(fused_kernel, n_ctx, n_head),
        in_specs=[pl.BlockSpec(memory_space=pltpu.SMEM), vmem, hbm, hbm, vmem, vmem],
        out_specs=[hbm, vmem],
        out_shape=[
            jax.ShapeDtypeStruct((heads, feat, toks), BF16),
            jax.ShapeDtypeStruct((part, feat), BF16),
        ],
        scratch_shapes=[
            pltpu.VMEM((steps, group, feat, toks), BF16),
            pltpu.VMEM((chunks, width, heads, lat), BF16),
            pltpu.VMEM((lat // 128, width * heads, 128), F32),
            pltpu.VMEM((steps, group, toks, lat), BF16),
            pltpu.VMEM((steps, keys, cols), BF16),
            pltpu.VMEM((steps, near, cols), BF16),
            pltpu.VMEM((steps, group, feat, toks), BF16),
            pltpu.VMEM((keys, feat), F32),
            pltpu.VMEM((n_off, n_head, part, feat), BF16),
            pltpu.VMEM((n_head - 1, n_off, part, feat), BF16),
            pltpu.VMEM((n_head - 1, n_off, part, feat), BF16),
            pltpu.VMEM((n_off - 1, part, feat), BF16),
            pltpu.VMEM((n_off - 1, part, feat), BF16),
            dma((steps,)),
            dma((chunks,)),
            dma((steps,)),
            dma((n_off - 1,)),
            dma((n_off - 1,)),
            dma((n_off, n_head - 1)),
            dma((n_off, n_head - 1)),
            dma((2, n_head - 1)),
            dma((2, n_head - 1)),
            dma((n_off - 1,)),
            dma((n_off - 1,)),
        ],
        compiler_params=pltpu.CompilerParams(
            collective_id=0, has_side_effects=True, vmem_limit_bytes=56 << 20
        ),
        cost_estimate=pl.CostEstimate(flops=12 * 10**9, bytes_accessed=14 * 10**6, transcendentals=2 * 10**6),
        name="mla_bwd",
    )(links, kv, q, g, ln.reshape(steps, group, toks), od.reshape(steps, group, toks))


def shards(q, g, ln, od, kv, links):
    dq, dkv = fused(
        lax.axis_size("ctx"),
        lax.axis_size("head"),
        jnp.transpose(q, (1, 2, 0)),
        g,
        ln.T,
        od.T,
        kv,
        links,
    )
    return jnp.transpose(dq, (2, 0, 1)), dkv


def solution(mesh):
    in_specs = (
        P("ctx", "head", None),
        P("ctx", "head", None),
        P("ctx", "head"),
        P("ctx", "head"),
        P(("ctx", "head"), None),
        P("ctx", None),
    )
    out_specs = (P("ctx", "head", None), P(("ctx", "head"), None))
    return jax.shard_map(shards, mesh=mesh, in_specs=in_specs, out_specs=out_specs, check_vma=False)
```

profile of v0, /device:TPU:0, one launch (start us, length us, event | category | flops | bytes accessed | tf_op | source)
XLA Modules:
  0.0 52.2 jit_solution(14560157216938017852)
XLA Ops:
  0.6 46.1 %mla_bwd.1 = (bf16[32,576,128]{2,1,0:T(8,128)(2,1)}, bf16[64,576]{1,0:T(8,128)(2,1)}) custom-call(s32[1,4]{1,0:T(1,128)} %links.1, bf16[64,576]{1,0:T(8,128)(2,1)} %kv_ref.1, bf16[32,576,128]{2,1,0:T(8,128)(2,1)} %bitcast.9, bf16[128,32,512]{2,1,0:T(8,128)(2,1)} %g_hbm.1, f32[8,4,128]{2,1,0:T(4,128)} %bitcast.10, f32[8,4,128]{2,1,0:T(4,128)} %bitcast.11), custom_call_target="tpu_custom_call" | custom-call | flops 12000000000 | bytes 14000000 | tf_op jit(solution)/shard_map/mla_bwd/pallas_call | solution.py:252
  46.7 0.0 copy-start
  46.7 4.9 %copy.10 = bf16[128,32,576]{0,2,1:T(8,128)(2,1)} copy(bf16[128,32,576]{0,2,1:T(8,128)(2,1)} %bitcast.8) | data formatting | bytes 9437184
  51.6 0.0 copy-done
  51.6 0.6 %copy.11 = bf16[64,576]{1,0:T(8,128)(2,1)} copy(bf16[64,576]{1,0:T(8,128)(2,1)S(1)} %copy-done) | data formatting | bytes 147456
Async XLA Ops:
  46.7 4.9 %copy-start = (bf16[64,576]{1,0:T(8,128)(2,1)S(1)}, bf16[64,576]{1,0:T(8,128)(2,1)}, u32[]{:S(2)}) copy-start(bf16[64,576]{1,0:T(8,128)(2,1)} %get-tuple-element.9) | copy-start | bytes 221188
where the time goes:
time: 52.4 us; the launch traced here: 52.2 us
  Pallas kernels  46.1 us (88%)
  local copies, waits for them, and re-layouts  5.52 us (11%)
  between operations  0.65 us (1%)
    pallas_call x1, Pallas kernels, fused(): pl.pallas_call(functools.partial(fused_kernel, n_ctx, n_head), in_specs=[...  46.1 us
    unnamed x4, local copies, waits for them, and re-layouts  5.52 us

commit v1 on v0

--- a/solution.py
+++ b/solution.py
@@ -23,9 +23,9 @@
 
 def fused_kernel(
     n_ctx, n_head, links, kv_ref, q_hbm, g_hbm, ln_ref, od_ref,
-    dq_hbm, dkv_ref,
-    qv, graw, gwide, gv, dsv, pbv, dqv, acc, kvbuf, away, yrecv, fwd, crecv,
-    q_sem, g_sem, dq_sem, gs_s, gs_r, fw_s, fw_r, ry_s, ry_r, rc_s, rc_r,
+    dqv, dkv_ref,
+    qv, graw, gwide, gv, dsv, pbv, acc, kvbuf, away, yrecv, fwd, crecv,
+    q_sem, g_sem, gs_s, gs_r, fw_s, fw_r, ry_s, ry_r, rc_s, rc_r,
 ):
     me = lax.axis_index("ctx")
     head = lax.axis_index("head")
@@ -43,15 +43,12 @@
     def load_q(i):
         return pltpu.make_async_copy(q_hbm.at[pl.ds(i * group, group)], qv.at[i], q_sem.at[i])
 
-    def store_dq(i):
-        return pltpu.make_async_copy(dqv.at[i], dq_hbm.at[pl.ds(i * group, group)], dq_sem.at[i])
-
-    def loop(count, body):
+    def loop(count, body, start=0):
         def run(i, carry):
             body(i)
             return carry
 
-        lax.fori_loop(0, count, run, 0)
+        lax.fori_loop(start, count, run, 0)
 
     def at_ctx(by):
         return (lax.rem(me + by + n_ctx, n_ctx), head)
@@ -86,7 +83,7 @@
         ]
         for pos in range(n_off)
     ]
-    for copy in gather:
+    for copy in [gather[0]] + gather[:0:-1]:
         copy.start()
     for copy in spread[0]:
         copy.start()
@@ -105,7 +102,7 @@
                     c, pl.ds(h, width, stride=heads), :
                 ].astype(BF16)
 
-    loop(chunks, relayout)
+    loop(chunks - 1, relayout)
 
     def scores(i, low, high):
         keys = kvbuf[low:high].reshape((high - low) * blk, feat)
@@ -161,14 +158,31 @@
     ]
 
     acc[...] = jnp.zeros_like(acc)
-    for pos in range(1, n_off):
-        if pos == FIRST[1]:
-            arrive(spread, FIRST)
-            first_scores(loop, steps, load_q, scores, dsv, pbv, blk)
-        gather[pos - 1].wait_recv()
-        for copy in spread[pos]:
-            copy.start()
-    arrive(spread, LAST)
+
+    def onward(low, high):
+        for pos in range(low, high):
+            gather[pos - 1].wait_recv()
+            for copy in spread[pos]:
+                copy.start()
+
+    def arrive(low, high):
+        for pos in range(low, high):
+            for copy in spread[pos]:
+                copy.wait_recv()
+
+    def first(i):
+        load_q(i).wait()
+        pb, ds, _, _ = scores(i, *FIRST)
+        dsv[i, : FIRST[1] * blk, :] = ds
+        pbv[i] = pb
+
+    onward(1, FIRST[1])
+    loop(chunks, relayout, chunks - 1)
+    arrive(*FIRST)
+    loop(steps // 2, first)
+    onward(*LAST)
+    loop(steps, first, steps // 2)
+    arrive(*LAST)
 
     def second(i):
         pb, ds, q, g = scores(i, *LAST)
@@ -187,7 +201,6 @@
         dq = dot(keys, dsv[i], 0, 0).astype(BF16)
         for k in range(group):
             dqv[i, k] = dq[:, k * toks : (k + 1) * toks]
-        store_dq(i).start()
 
     far, near = across(*LAST, 1), across(*FIRST, 0)
     for copy in far:
@@ -210,7 +223,6 @@
     total = folded(0)
     for pos in range(1, FIRST[1]):
         back[pos - 1].start()
-    loop(steps, lambda i: store_dq(i).wait())
     for copy in gather + sum(spread, []) + far + near:
         copy.wait_send()
     for copy in back[::-1]:
@@ -218,22 +230,6 @@
     for pos in range(1, n_off):
         total = total + crecv[pos - 1].astype(F32)
     dkv_ref[...] = total.astype(BF16)
-
-
-def arrive(spread, span):
-    for pos in range(*span):
-        for copy in spread[pos]:
-            copy.wait_recv()
-
-
-def first_scores(loop, steps, load_q, scores, dsv, pbv, blk):
-    def first(i):
-        load_q(i).wait()
-        pb, ds, _, _ = scores(i, *FIRST)
-        dsv[i, : FIRST[1] * blk, :] = ds
-        pbv[i] = pb
-
-    loop(steps, first)
 
 
 def fused(n_ctx, n_head, q, g, ln, od, kv, links, group=4, width=32):
@@ -252,9 +248,9 @@
     return pl.pallas_call(
         functools.partial(fused_kernel, n_ctx, n_head),
         in_specs=[pl.BlockSpec(memory_space=pltpu.SMEM), vmem, hbm, hbm, vmem, vmem],
-        out_specs=[hbm, vmem],
+        out_specs=[vmem, vmem],
         out_shape=[
-            jax.ShapeDtypeStruct((heads, feat, toks), BF16),
+            pltpu.VMEM((steps, group, feat, toks), BF16),
             jax.ShapeDtypeStruct((part, feat), BF16),
         ],
         scratch_shapes=[
@@ -264,7 +260,6 @@
             pltpu.VMEM((steps, group, toks, lat), BF16),
             pltpu.VMEM((steps, keys, cols), BF16),
             pltpu.VMEM((steps, near, cols), BF16),
-            pltpu.VMEM((steps, group, feat, toks), BF16),
             pltpu.VMEM((keys, feat), F32),
             pltpu.VMEM((n_off, n_head, part, feat), BF16),
             pltpu.VMEM((n_head - 1, n_off, part, feat), BF16),
@@ -273,7 +268,6 @@
             pltpu.VMEM((n_off - 1, part, feat), BF16),
             dma((steps,)),
             dma((chunks,)),
-            dma((steps,)),
             dma((n_off - 1,)),
             dma((n_off - 1,)),
             dma((n_off, n_head - 1)),
@@ -284,7 +278,7 @@
             dma((n_off - 1,)),
         ],
         compiler_params=pltpu.CompilerParams(
-            collective_id=0, has_side_effects=True, vmem_limit_bytes=56 << 20
+            collective_id=0, has_side_effects=True, vmem_limit_bytes=67043328 - 2 * heads * feat * toks - 16384
         ),
         cost_estimate=pl.CostEstimate(flops=12 * 10**9, bytes_accessed=14 * 10**6, transcendentals=2 * 10**6),
         name="mla_bwd",
@@ -302,7 +296,7 @@
         kv,
         links,
     )
-    return jnp.transpose(dq, (2, 0, 1)), dkv
+    return jnp.transpose(dq.reshape(-1, *dq.shape[2:]), (2, 0, 1)), dkv
 
 
 def solution(mesh):

time: 52.4 us -> 45.8 us (0.87)
  Pallas kernels: 46.1 us -> 42.1 us
  local copies, waits for them, and re-layouts: 5.52 us -> 2.83 us
    pallas_call x1, Pallas kernels: 46.1 us -> 42.1 us  [fused(): pl.pallas_call(functools.partial(fused_kernel, n_ctx, n_head), in_specs=[...]
    unnamed x4, local copies, waits for them, and re-layouts: 5.52 us -> 2.83 us
where the time goes in v1:
time: 45.8 us; the launch traced here: 45.6 us
  Pallas kernels  42.1 us (92%)
  local copies, waits for them, and re-layouts  2.83 us (6%)
  between operations  0.65 us (1%)
    pallas_call x1, Pallas kernels, fused(): pl.pallas_call(functools.partial(fused_kernel, n_ctx, n_head), in_specs=[...  42.1 us
    unnamed x4, local copies, waits for them, and re-layouts  2.83 us

profile of v1, /device:TPU:0, one launch (start us, length us, event | category | flops | bytes accessed | tf_op | source)
XLA Modules:
  0.0 45.6 jit_solution(17050894799397144408)
XLA Ops:
  0.6 42.1 %mla_bwd.1 = (bf16[8,4,576,128]{3,2,1,0:T(8,128)(2,1)S(1)}, bf16[64,576]{1,0:T(8,128)(2,1)}) custom-call(s32[1,4]{1,0:T(1,128)} %links.1, bf16[64,576]{1,0:T(8,128)(2,1)} %kv_ref.1, bf16[32,576,128]{2,1,0:T(8,128)(2,1)} %bitcast.11, bf16[128,32,512]{2,1,0:T(8,128)(2,1)} %g_hbm.1, f32[8,4,128]{2,1,0:T(4,128)} %bitcast.12, f32[8,4,128]{2,1,0:T(4,128)} %bitcast.13), custom_call_target="tpu_custom_call" | custom-call | flops 12000000000 | bytes 14000000 | tf_op jit(solution)/shard_map/mla_bwd/pallas_call | solution.py:248
  42.8 0.0 copy-start
  42.8 2.2 %copy.10 = bf16[128,32,576]{0,2,1:T(8,128)(2,1)} copy(bf16[128,32,576]{0,2,1:T(8,128)(2,1)S(1)} %bitcast.10) | data formatting | bytes 9437184
  45.0 0.0 copy-done
  45.0 0.6 %copy.11 = bf16[64,576]{1,0:T(8,128)(2,1)} copy(bf16[64,576]{1,0:T(8,128)(2,1)S(1)} %copy-done) | data formatting | bytes 147456
Async XLA Ops:
  42.8 2.2 %copy-start = (bf16[64,576]{1,0:T(8,128)(2,1)S(1)}, bf16[64,576]{1,0:T(8,128)(2,1)}, u32[]{:S(2)}) copy-start(bf16[64,576]{1,0:T(8,128)(2,1)} %get-tuple-element.11) | copy-start | bytes 221188

commit v2 on v1

--- a/solution.py
+++ b/solution.py
@@ -232,7 +232,7 @@
     dkv_ref[...] = total.astype(BF16)
 
 
-def fused(n_ctx, n_head, q, g, ln, od, kv, links, group=4, width=32):
+def fused(n_ctx, n_head, q, g, ln, od, kv, links, group=8, width=32):
     heads, feat, toks = q.shape
     lat = g.shape[2]
     part = kv.shape[0]

time: 45.8 us -> 44.2 us (0.965)
  Pallas kernels: 42.1 us -> 40.5 us
    pallas_call x1, Pallas kernels: 42.1 us -> 40.5 us  [fused(): pl.pallas_call(functools.partial(fused_kernel, n_ctx, n_head), in_specs=[...]
where the time goes in v2:
time: 44.2 us; the launch traced here: 44 us
  Pallas kernels  40.5 us (92%)
  local copies, waits for them, and re-layouts  2.83 us (6%)
  between operations  0.65 us (1%)
    pallas_call x1, Pallas kernels, fused(): pl.pallas_call(functools.partial(fused_kernel, n_ctx, n_head), in_specs=[...  40.5 us
    unnamed x4, local copies, waits for them, and re-layouts  2.83 us

profile of v2, /device:TPU:0, one launch (start us, length us, event | category | flops | bytes accessed | tf_op | source)
XLA Modules:
  0.0 44.0 jit_solution(10614576024629145587)
XLA Ops:
  0.6 40.5 %mla_bwd.1 = (bf16[4,8,576,128]{3,2,1,0:T(8,128)(2,1)S(1)}, bf16[64,576]{1,0:T(8,128)(2,1)}) custom-call(s32[1,4]{1,0:T(1,128)} %links.1, bf16[64,576]{1,0:T(8,128)(2,1)} %kv_ref.1, bf16[32,576,128]{2,1,0:T(8,128)(2,1)} %bitcast.11, bf16[128,32,512]{2,1,0:T(8,128)(2,1)} %g_hbm.1, f32[4,8,128]{2,1,0:T(8,128)} %bitcast.12, f32[4,8,128]{2,1,0:T(8,128)} %bitcast.13), custom_call_target="tpu_custom_call" | custom-call | flops 12000000000 | bytes 14000000 | tf_op jit(solution)/shard_map/mla_bwd/pallas_call | solution.py:248
  41.2 0.0 copy-start
  41.2 2.2 %copy.10 = bf16[128,32,576]{0,2,1:T(8,128)(2,1)} copy(bf16[128,32,576]{0,2,1:T(8,128)(2,1)S(1)} %bitcast.10) | data formatting | bytes 9437184
  43.4 0.0 copy-done
  43.4 0.6 %copy.11 = bf16[64,576]{1,0:T(8,128)(2,1)} copy(bf16[64,576]{1,0:T(8,128)(2,1)S(1)} %copy-done) | data formatting | bytes 147456
Async XLA Ops:
  41.2 2.2 %copy-start = (bf16[64,576]{1,0:T(8,128)(2,1)S(1)}, bf16[64,576]{1,0:T(8,128)(2,1)}, u32[]{:S(2)}) copy-start(bf16[64,576]{1,0:T(8,128)(2,1)} %get-tuple-element.11) | copy-start | bytes 221188
